TPU v7x, 32 devices: a whole 2x2x4 slice. The times are simulated.
32 devices in a mesh: dp: 4 (over z), blk: 2 (over x), ulys: 4 (over y, core).
Axes of the slice: x: 2, y: 2, z: 4, core: 2. Of those that a mesh axis runs over, the one named last changes fastest.
Arguments:
- hidden: float32 [6144, 768], P(('dp', 'blk', 'ulys')), may hold values from -6 to 6
- time_embed: float32 [4, 768], P('dp'), may hold values from -6 to 6
- segment_ids: int32 [4, 1536], P('dp', 'blk'), may hold values from 0 to 7, never falling along the last dimension, each value on 1 to 384 neighbouring positions
- key_valid: int32 [4, 1536], P('dp', 'blk'), may hold values 0 or 1
- out_grad: float32 [6144, 768], P(('dp', 'blk', 'ulys')), may hold values from -6 to 6
- w_query: float32 [768, 768], P(('blk', 'ulys')), may hold values from -0.21875 to 0.21875
- b_query: float32 [768], P(('blk', 'ulys')), may hold values from -3 to 3
- w_key: float32 [768, 768], P(('blk', 'ulys')), may hold values from -0.21875 to 0.21875
- w_value: float32 [768, 768], P(('blk', 'ulys')), may hold values from -0.21875 to 0.21875
- b_value: float32 [768], P(('blk', 'ulys')), may hold values from -3 to 3
- w_out: float32 [768, 768], P(('blk', 'ulys')), may hold values from -3 to 3
- b_out: float32 [768], P(('blk', 'ulys')), may hold values from -3 to 3
- w_up: float32 [768, 3072], P(('blk', 'ulys')), may hold values from -0.21875 to 0.21875
- b_up: float32 [3072], P(('blk', 'ulys')), may hold values from -3 to 3
- w_down: float32 [3072, 768], P(('blk', 'ulys')), may hold values from -0.109375 to 0.109375
- b_down: float32 [768], P(('blk', 'ulys')), may hold values from -3 to 3
- pre_gain: float32 [768], P(('blk', 'ulys')), may hold values from 0.5 to 1.5
- pre_shift: float32 [768], P(('blk', 'ulys')), may hold values from -3 to 3
- mlp_gain: float32 [768], P(('blk', 'ulys')), may hold values from 0.5 to 1.5
- mlp_shift: float32 [768], P(('blk', 'ulys')), may hold values from -3 to 3
Outputs:
- output: float32 [6144, 768], P(('dp', 'blk', 'ulys'))
- hidden_grad: float32 [6144, 768], P(('dp', 'blk', 'ulys'))
- grad_query: float32 [768, 768], P(('blk', 'ulys'))
- grad_qbias: float32 [768], P(('blk', 'ulys'))
- grad_key: float32 [768, 768], P(('blk', 'ulys'))
- grad_value: float32 [768, 768], P(('blk', 'ulys'))
- grad_vbias: float32 [768], P(('blk', 'ulys'))
- grad_outproj: float32 [768, 768], P(('blk', 'ulys'))
- grad_obias: float32 [768], P(('blk', 'ulys'))
- grad_upproj: float32 [768, 3072], P(('blk', 'ulys'))
- grad_upbias: float32 [3072], P(('blk', 'ulys'))
- grad_downproj: float32 [3072, 768], P(('blk', 'ulys'))
- grad_downbias: float32 [768], P(('blk', 'ulys'))
- prenorm_gain_gradient: float32 [768], P(('blk', 'ulys'))
- prenorm_shift_gradient: float32 [768], P(('blk', 'ulys'))
- grad_mlpgain: float32 [768], P(('blk', 'ulys'))
- grad_mlpshift: float32 [768], P(('blk', 'ulys'))
Inputs may be any that keep to these rules, and one draw needn't show every extreme that they name: `segment_ids`: segment ids never fall along a sequence; a document holds at most 384 tokens, and some document of each sequence holds exactly that many.
All inputs are finite; a program needn't handle non-finite values. No bound on the sum of `key_valid` on one device may be relied on, other than what follows from the above.
Results may differ from a plain program's by a relative error of at most 0.0003.
Values sent between devices are 32-bit elements; how exact they have to be, the bound alone decides.
No kernel may reach another device: no remote copies, remote signals or barrier semaphores. Data moves between devices by JAX's collectives and lax.ppermute only.
A program may use at most 192 MiB of HBM per device.

v0:
```python
import math
import jax
import jax.numpy as jnp
from jax import lax
from jax.sharding import PartitionSpec as P

HEAD_DIM = 64
HIGH = lax.Precision.HIGHEST
floor_score = -1e30


def layer_normalize(values, gain, shift):
    average = jnp.mean(values, axis=-1, keepdims=True)
    centred = values - average
    variance = jnp.mean(centred * centred, axis=-1, keepdims=True)
    return centred * lax.rsqrt(variance + 1e-05) * gain + shift


def gelu_tanh(values):
    return (
        0.5
        * values
        * (1.0 + jnp.tanh(0.7978845608028654 * (values + 0.044715 * values * values * values)))
    )


def matmul(left, right):
    return jnp.dot(left, right, precision=HIGH)


def matmul_left_t(left, right):
    return lax.dot_general(left, right, (((0,), (0,)), ((), ())), precision=HIGH)


def matmul_right_t(left, right):
    return lax.dot_general(left, right, (((1,), (1,)), ((), ())), precision=HIGH)


def local(
    hidden,
    time_embed,
    segment_ids,
    key_valid,
    out_grad,
    w_query,
    b_query,
    w_key,
    w_value,
    b_value,
    w_out,
    b_out,
    w_up,
    b_up,
    w_down,
    b_down,
    pre_gain,
    pre_shift,
    mlp_gain,
    mlp_shift,
):
    (
        full_query,
        full_qbias,
        full_key,
        full_value,
        full_vbias,
        full_out,
        full_obias,
        full_up,
        full_upbias,
        full_down,
        full_downbias,
        complete_prenorm_gain,
        complete_prenorm_shift,
        full_mlpgain,
        full_mlpshift,
    ) = (
        lax.all_gather(w_query, ("blk", "ulys"), axis=0, tiled=True),
        lax.all_gather(b_query, ("blk", "ulys"), axis=0, tiled=True),
        lax.all_gather(w_key, ("blk", "ulys"), axis=0, tiled=True),
        lax.all_gather(w_value, ("blk", "ulys"), axis=0, tiled=True),
        lax.all_gather(b_value, ("blk", "ulys"), axis=0, tiled=True),
        lax.all_gather(w_out, ("blk", "ulys"), axis=0, tiled=True),
        lax.all_gather(b_out, ("blk", "ulys"), axis=0, tiled=True),
        lax.all_gather(w_up, ("blk", "ulys"), axis=0, tiled=True),
        lax.all_gather(b_up, ("blk", "ulys"), axis=0, tiled=True),
        lax.all_gather(w_down, ("blk", "ulys"), axis=0, tiled=True),
        lax.all_gather(b_down, ("blk", "ulys"), axis=0, tiled=True),
        lax.all_gather(pre_gain, ("blk", "ulys"), axis=0, tiled=True),
        lax.all_gather(pre_shift, ("blk", "ulys"), axis=0, tiled=True),
        lax.all_gather(mlp_gain, ("blk", "ulys"), axis=0, tiled=True),
        lax.all_gather(mlp_shift, ("blk", "ulys"), axis=0, tiled=True),
    )
    residual_input = hidden + time_embed
    normalized_rows, prenorm_backward = jax.vjp(
        layer_normalize, residual_input, complete_prenorm_gain, complete_prenorm_shift
    )
    query = matmul(normalized_rows, full_query) + full_qbias
    keys = matmul(normalized_rows, full_key)
    values = matmul(normalized_rows, full_value) + full_vbias
    query_heads, key_heads, value_heads = (
        lax.all_to_all(query, "ulys", split_axis=1, concat_axis=0, tiled=True),
        lax.all_to_all(keys, "ulys", split_axis=1, concat_axis=0, tiled=True),
        lax.all_to_all(values, "ulys", split_axis=1, concat_axis=0, tiled=True),
    )
    group = query_heads.shape[0]
    width = query_heads.shape[1]
    heads_here = width // HEAD_DIM
    blk_count = lax.axis_size("blk")
    blk_here = lax.axis_index("blk")
    length = group * blk_count
    scale = HEAD_DIM ** (-0.5)
    segments_here = segment_ids[0]
    query_codes = segments_here.astype(jnp.float32)
    key_codes = jnp.where(key_valid[0] == 1, segments_here, -1).astype(jnp.float32)
    query_rows = blk_here * group + jnp.arange(group, dtype=jnp.int32)
    query_split = query_heads.reshape(group, heads_here, HEAD_DIM)
    key_value = jnp.concatenate([key_heads, value_heads], axis=1)

    def block_scores(kv_block, code_block, key_rows):
        key_split = kv_block[:, :width].reshape(-1, heads_here, HEAD_DIM)
        value_split = kv_block[:, width:].reshape(-1, heads_here, HEAD_DIM)
        scores = jnp.einsum("qhd,khd->hqk", query_split, key_split, precision=HIGH) * scale
        allowed = (query_codes[:, None] == code_block[None, :]) | (
            query_rows[:, None] == key_rows[None, :]
        )
        return (scores, allowed[None], key_split, value_split)

    def over_blocks(state, piece, update):
        kv_piece, code_piece = piece
        rows = kv_piece.shape[0]
        size = math.gcd(rows, group)
        count = rows // size
        kv_blocks = kv_piece.reshape(count, size, kv_piece.shape[1])
        code_blocks = code_piece.reshape(count, size)
        offsets = jnp.arange(count, dtype=jnp.int32) * size

        def visit(carried, item):
            kv_block, code_block, offset = item
            key_rows = offset + jnp.arange(size, dtype=jnp.int32)
            carried = update(carried, kv_block, code_block, key_rows)
            return (carried, None)

        state, unused = lax.scan(visit, state, (kv_blocks, code_blocks, offsets))
        return state

    def forward_update(state, kv_block, code_block, key_rows):
        running_max, total, accum = state
        scores, allowed, key_split, value_split = block_scores(kv_block, code_block, key_rows)
        masked = jnp.where(allowed, scores, floor_score)
        new_max = jnp.maximum(running_max, jnp.max(masked, axis=2))
        weights = jnp.where(allowed, jnp.exp(masked - new_max[:, :, None]), 0.0)
        factor = jnp.exp(running_max - new_max)
        total = total * factor + jnp.sum(weights, axis=2)
        weighted = jnp.einsum("hqk,khd->qhd", weights, value_split, precision=HIGH)
        accum = accum.reshape(group, heads_here, HEAD_DIM) * factor.T[:, :, None] + weighted
        return (new_max, total, accum.reshape(group, width))

    start_state = (
        jnp.full((heads_here, group), floor_score, jnp.float32),
        jnp.zeros((heads_here, group), jnp.float32),
        jnp.zeros((group, width), jnp.float32),
    )
    running_max, total, accum = over_blocks(
        start_state,
        (
            lax.all_gather(key_value, "blk", axis=0, tiled=True),
            lax.all_gather(key_codes, "blk", axis=0, tiled=True),
        ),
        forward_update,
    )
    normalizer = running_max + jnp.log(total)
    attended_heads = (accum.reshape(group, heads_here, HEAD_DIM) / total.T[:, :, None]).reshape(
        group, width
    )
    attended = lax.all_to_all(attended_heads, "ulys", split_axis=0, concat_axis=1, tiled=True)
    middle = residual_input + matmul(attended, full_out) + full_obias
    mlp_in, mlp_back = jax.vjp(layer_normalize, middle, full_mlpgain, full_mlpshift)
    pre_act = matmul(mlp_in, full_up) + full_upbias
    activated, gelu_back = jax.vjp(gelu_tanh, pre_act)
    output = middle + matmul(activated, full_down) + full_downbias
    back_query, back_key, back_value, back_out, back_up, back_down = (
        lax.all_gather(w_query, ("blk", "ulys"), axis=0, tiled=True),
        lax.all_gather(w_key, ("blk", "ulys"), axis=0, tiled=True),
        lax.all_gather(w_value, ("blk", "ulys"), axis=0, tiled=True),
        lax.all_gather(w_out, ("blk", "ulys"), axis=0, tiled=True),
        lax.all_gather(w_up, ("blk", "ulys"), axis=0, tiled=True),
        lax.all_gather(w_down, ("blk", "ulys"), axis=0, tiled=True),
    )
    grad_downbias = jnp.sum(out_grad, axis=0)
    grad_downproj = matmul_left_t(activated, out_grad)
    act_grad = matmul_right_t(out_grad, back_down)
    (pre_grad,) = gelu_back(act_grad)
    grad_upproj = matmul_left_t(mlp_in, pre_grad)
    grad_upbias = jnp.sum(pre_grad, axis=0)
    mlp_in_grad = matmul_right_t(pre_grad, back_up)
    middle_part, grad_mlpgain, grad_mlpshift = mlp_back(mlp_in_grad)
    middle_grad = out_grad + middle_part
    grad_outproj = matmul_left_t(attended, middle_grad)
    grad_obias = jnp.sum(middle_grad, axis=0)
    attended_grad = matmul_right_t(middle_grad, back_out)
    grad_heads = lax.all_to_all(attended_grad, "ulys", split_axis=1, concat_axis=0, tiled=True)
    grad_split = grad_heads.reshape(group, heads_here, HEAD_DIM)
    row_dots = jnp.sum(grad_split * attended_heads.reshape(group, heads_here, HEAD_DIM), axis=2).T

    def backward_from(first_row):

        def backward_update(state, kv_block, code_block, key_rows):
            query_grad, pair_grads = state
            scores, allowed, key_split, value_split = block_scores(kv_block, code_block, key_rows)
            weights = jnp.exp(jnp.where(allowed, scores - normalizer[:, :, None], floor_score))
            values_grad = jnp.einsum("hqk,qhd->khd", weights, grad_split, precision=HIGH)
            weights_grad = jnp.einsum("qhd,khd->hqk", grad_split, value_split, precision=HIGH)
            score_grad = weights * (weights_grad - row_dots[:, :, None]) * scale
            query_grad = query_grad + jnp.einsum(
                "hqk,khd->qhd", score_grad, key_split, precision=HIGH
            ).reshape(group, width)
            keys_grad = jnp.einsum("hqk,qhd->khd", score_grad, query_split, precision=HIGH)
            size = key_rows.shape[0]
            block_grad = jnp.concatenate(
                [keys_grad.reshape(size, width), values_grad.reshape(size, width)], axis=1
            )
            place = key_rows[0] - first_row
            current = lax.dynamic_slice_in_dim(pair_grads, place, size, 0)
            pair_grads = lax.dynamic_update_slice_in_dim(pair_grads, current + block_grad, place, 0)
            return (query_grad, pair_grads)

        return backward_update

    back_state = (
        jnp.zeros((group, width), jnp.float32),
        jnp.zeros((length, 2 * width), jnp.float32),
    )
    query_grad, pair_grads = over_blocks(
        back_state,
        (
            lax.all_gather(key_value, "blk", axis=0, tiled=True),
            lax.all_gather(key_codes, "blk", axis=0, tiled=True),
        ),
        backward_from(0),
    )
    local_pairs = lax.psum_scatter(pair_grads, "blk", scatter_dimension=0, tiled=True)
    token_query_grad, token_keys_grad, token_values_grad = (
        lax.all_to_all(query_grad, "ulys", split_axis=0, concat_axis=1, tiled=True),
        lax.all_to_all(local_pairs[:, :width], "ulys", split_axis=0, concat_axis=1, tiled=True),
        lax.all_to_all(local_pairs[:, width:], "ulys", split_axis=0, concat_axis=1, tiled=True),
    )
    grad_query = matmul_left_t(normalized_rows, token_query_grad)
    grad_qbias = jnp.sum(token_query_grad, axis=0)
    grad_key = matmul_left_t(normalized_rows, token_keys_grad)
    grad_value = matmul_left_t(normalized_rows, token_values_grad)
    grad_vbias = jnp.sum(token_values_grad, axis=0)
    normalized_gradient = (
        matmul_right_t(token_query_grad, back_query)
        + matmul_right_t(token_keys_grad, back_key)
        + matmul_right_t(token_values_grad, back_value)
    )
    residual_slice, prenorm_gain_gradient, prenorm_shift_gradient = prenorm_backward(
        normalized_gradient
    )
    hidden_grad = middle_grad + residual_slice
    shard_sums = (
        lax.psum_scatter(grad_query, ("blk", "ulys"), scatter_dimension=0, tiled=True),
        lax.psum_scatter(grad_qbias, ("blk", "ulys"), scatter_dimension=0, tiled=True),
        lax.psum_scatter(grad_key, ("blk", "ulys"), scatter_dimension=0, tiled=True),
        lax.psum_scatter(grad_value, ("blk", "ulys"), scatter_dimension=0, tiled=True),
        lax.psum_scatter(grad_vbias, ("blk", "ulys"), scatter_dimension=0, tiled=True),
        lax.psum_scatter(grad_outproj, ("blk", "ulys"), scatter_dimension=0, tiled=True),
        lax.psum_scatter(grad_obias, ("blk", "ulys"), scatter_dimension=0, tiled=True),
        lax.psum_scatter(grad_upproj, ("blk", "ulys"), scatter_dimension=0, tiled=True),
        lax.psum_scatter(grad_upbias, ("blk", "ulys"), scatter_dimension=0, tiled=True),
        lax.psum_scatter(grad_downproj, ("blk", "ulys"), scatter_dimension=0, tiled=True),
        lax.psum_scatter(grad_downbias, ("blk", "ulys"), scatter_dimension=0, tiled=True),
        lax.psum_scatter(prenorm_gain_gradient, ("blk", "ulys"), scatter_dimension=0, tiled=True),
        lax.psum_scatter(prenorm_shift_gradient, ("blk", "ulys"), scatter_dimension=0, tiled=True),
        lax.psum_scatter(grad_mlpgain, ("blk", "ulys"), scatter_dimension=0, tiled=True),
        lax.psum_scatter(grad_mlpshift, ("blk", "ulys"), scatter_dimension=0, tiled=True),
    )
    totals = lax.psum(
        (
            shard_sums[0],
            shard_sums[1],
            shard_sums[2],
            shard_sums[3],
            shard_sums[4],
            shard_sums[5],
            shard_sums[6],
            shard_sums[7],
            shard_sums[8],
            shard_sums[9],
            shard_sums[10],
            shard_sums[11],
            shard_sums[12],
            shard_sums[13],
            shard_sums[14],
        ),
        "dp",
    )
    return (output, hidden_grad) + tuple(totals)


def solution(mesh):
    placed = (
        P(("dp", "blk", "ulys"), None),
        P("dp", None),
        P("dp", "blk"),
        P("dp", "blk"),
        P(("dp", "blk", "ulys"), None),
        P(("blk", "ulys"), None),
        P(("blk", "ulys")),
        P(("blk", "ulys"), None),
        P(("blk", "ulys"), None),
        P(("blk", "ulys")),
        P(("blk", "ulys"), None),
        P(("blk", "ulys")),
        P(("blk", "ulys"), None),
        P(("blk", "ulys")),
        P(("blk", "ulys"), None),
        P(("blk", "ulys")),
        P(("blk", "ulys")),
        P(("blk", "ulys")),
        P(("blk", "ulys")),
        P(("blk", "ulys")),
    )
    return jax.shard_map(
        local,
        mesh=mesh,
        in_specs=placed,
        out_specs=(
            P(("dp", "blk", "ulys"), None),
            P(("dp", "blk", "ulys"), None),
            P(("blk", "ulys"), None),
            P(("blk", "ulys")),
            P(("blk", "ulys"), None),
            P(("blk", "ulys"), None),
            P(("blk", "ulys")),
            P(("blk", "ulys"), None),
            P(("blk", "ulys")),
            P(("blk", "ulys"), None),
            P(("blk", "ulys")),
            P(("blk", "ulys"), None),
            P(("blk", "ulys")),
            P(("blk", "ulys")),
            P(("blk", "ulys")),
            P(("blk", "ulys")),
            P(("blk", "ulys")),
        ),
        check_vma=False,
    )
```

profile of v0, /device:TPU:0, one launch (start us, length us, event | category | flops | bytes accessed | tf_op | source)
XLA Modules:
  0.0 1022.3 jit_solution(7947573977653093022)
XLA Ops:
  18.0 26.4 %all-reduce.18 = (f32[768]{0:T(1024)S(1)}, f32[768]{0:T(1024)S(1)}, f32[768]{0:T(1024)S(1)}, f32[768]{0:T(1024)}, f32[768]{0:T(1024)}, /*index=5*/f32[768]{0:T(1024)}, f32[768]{0:T(1024)}) all-reduce(f32[768]{0:T(1024)S(1)} %dynamic-update-slice.2, ...), channel_id=1, replica_groups=mesh['dp'=4,'blk'=2,'ulys'=4] {'blk','ulys'}, use_global_device_ids=true, to_apply=%add.2 | all-reduce | flops 5376 | bytes 43008
  55.1 19.6 %all-gather.10.cloned.1.call-done = f32[768,768]{1,0:T(8,128)} async-done(((f32[96,768]{1,0:T(8,128)}), f32[768,768]{1,0:T(8,128)}) %all-gather.10.cloned.1.call-update) | async-done | bytes 2359312 | tf_op jit(solution)/shard_map/all_gather | solution.py:80
  74.7 6.5 fusion.62
  85.7 12.1 %all-to-all-done = f32[192,4,192]{0,2,1:T(8,128)S(1)} async-done(((f32[192,4,192]{0,2,1:T(8,128)}), f32[192,4,192]{0,2,1:T(8,128)S(1)}, u32[]{:S(2)}, u32[]{:S(2)}) %all-to-all-start) | async-done | bytes 589856 | tf_op jit(solution)/shard_map/all_to_all | solution.py:103
  101.9 6.2 all-gather.16.cloned.1.call-done
  122.9 5.5 all-to-all-done.2
  129.3 16.9 %all-gather.14.cloned.1.call-done = f32[1536,384]{0,1:T(8,128)} async-done(((f32[768,384]{0,1:T(8,128)}), f32[1536,384]{0,1:T(8,128)}) %all-gather.14.cloned.1.call-update) | async-done | bytes 2359312 | tf_op jit(solution)/shard_map/all_gather | solution.py:167
  150.3 49.9 %while.28 = (s32[]{:T(128)}, f32[3,768]{1,0:T(4,128)S(1)}, f32[3,768]{1,0:T(4,128)}, f32[768,192]{0,1:T(8,128)S(1)}, f32[768]{0:T(1024)}, /*index=5*/f32[2,768]{...) while((s32[]{:T(128)}, f32[3,768]{1,0:T(4,128)S(1)}, ...), condition=%wide.region_5.6_spmd.clone, body=%wide.region_2.5_spmd.clone.sunk | while | flops 2741222400 | bytes 31506652 | solution.py:144
  155.6 6.9 fusion.146
  162.5 6.2 fusion.150
  176.3 6.9 fusion.146
  183.3 6.2 fusion.150
  205.9 22.6 %all-gather.1 = f32[8,1,384]{2,1,0:T(1,128)} all-gather(f32[1,1,384]{2,1,0:T(1,128)S(1)} %reshape.337), channel_id=1, replica_groups=mesh['dp'=4,'blk'=2,'ulys'=4] {'blk','ulys'}, dimensions={0}, use_global_device_ids=true | all-gather | bytes 13824 | tf_op jit(solution)/shard_map/all_gather | solution.py:86
  234.9 10.0 all-gather.20.cloned.1.call-done
  244.9 9.0 convolution_add_fusion
  254.0 50.8 %all-gather.22.cloned.1.call-done = f32[3072,768]{1,0:T(8,128)} async-done(((f32[384,768]{1,0:T(8,128)}), f32[3072,768]{1,0:T(8,128)}) %all-gather.22.cloned.1.call-update) | async-done | bytes 9437200 | tf_op jit(solution)/shard_map/all_gather | solution.py:87
  304.7 14.4 %fusion.64 = (f32[3072]{0:T(1024)}, f32[192,3072]{1,0:T(8,128)S(1)}) fusion(f32[192,3072]{1,0:T(8,128)S(1)} %convolution_add_fusion, f32[192,768]{1,0:T(8,128)} %param.28, f32[3072,768]{1,0:T(8,128)} %all-gather.22.cloned.1.call-done), kind=kOutput, calls=%fused_computation.123 | convolution fusion | flops 5449970688 | bytes 14757888 | tf_op jit(solution)/shard_map/dot_general | solution.py:36
  319.2 10.1 multiply_reduce_fusion
  340.4 11.0 %all-to-all-done.4 = f32[192,4,192]{2,0,1:T(8,128)} async-done(((f32[192,4,192]{2,0,1:T(8,128)}), f32[192,4,192]{2,0,1:T(8,128)}, u32[]{:S(2)}, u32[]{:S(2)}) %all-to-all-start.4) | async-done | bytes 589856 | tf_op jit(solution)/shard_map/all_to_all | solution.py:202
  357.8 123.8 %while.29 = (s32[]{:T(128)}, f32[768,192]{0,1:T(8,128)S(1)}, f32[1536,384]{0,1:T(8,128)}, f32[2,768,384]{1,2,0:T(8,128)}, f32[768]{0:T(1024)S(1)}, /*index=5*/f3...) while((s32[]{:T(128)}, f32[768,192]{0,1:T(8,128)S(1)}, ...), condition=%wide.region_12.13_spmd.clone, body=%wide.region_11.12_spmd.clone.sunk | while | flops 6813353472 | bytes 72011080 | solution.py:144
  384.6 6.0 fusion.162
  390.5 8.8 fusion.165
  399.4 8.7 fusion.163
  412.4 6.9 fusion.166
  419.8 6.8 dynamic_update_slice.5
  433.0 6.0 fusion.162
  439.0 8.8 fusion.165
  447.8 8.7 fusion.163
  460.8 6.9 fusion.166
  468.3 6.1 dynamic_update_slice.5
  486.8 14.1 %all_to_all.146 = f32[4,192,192]{2,1,0:T(8,128)S(1)} all-to-all(f32[4,192,192]{2,1,0:T(8,128)S(1)} %bitcast.210), channel_id=1, replica_groups=mesh['dp'=4,'blk'=2,'ulys'=4] {'ulys'}, dimensions={0} | all-to-all | bytes 1179648 | tf_op jit(solution)/shard_map/all_to_all | solution.py:244
  506.5 10.0 reduce-scatter.8.cloned.1.call-done
  518.1 14.2 %all_to_all.147 = f32[4,192,192]{2,1,0:T(8,128)S(1)} all-to-all(f32[4,192,192]{2,1,0:T(8,128)S(1)} %bitcast.211), channel_id=1, replica_groups=mesh['dp'=4,'blk'=2,'ulys'=4] {'ulys'}, dimensions={0} | all-to-all | bytes 1179648 | tf_op jit(solution)/shard_map/all_to_all | solution.py:246
  538.2 20.1 %all_to_all.148 = f32[4,192,192]{2,1,0:T(8,128)S(1)} all-to-all(f32[4,192,192]{2,1,0:T(8,128)S(1)} %bitcast.212), channel_id=1, replica_groups=mesh['dp'=4,'blk'=2,'ulys'=4] {'ulys'}, dimensions={0} | all-to-all | bytes 1179648 | tf_op jit(solution)/shard_map/all_to_all | solution.py:245
  560.1 4.9 fusion.60
  565.1 10.9 %fusion.37 = f32[768,3072]{1,0:T(8,128)} fusion(f32[192,3072]{1,0:T(8,128)S(1)} %copy-done.13, f32[192,768]{1,0:T(8,128)S(1)} %copy-done.6, f32[768]{0:T(1024)S(1)} %copy-done.36, f32[768]{0:T(1024)S(1)} %copy-done.35, f32[192]{0:T(256)} %fusion.50, f32[192]{0:T(256)} %copy-done.40), kind=kOutput, calls=%fused_computation.82 | convolution fusion | flops 5436407808 | bytes 12393984 | tf_op jit(solution)/shard_map/dot_general | solution.py:32
  577.7 11.7 %fusion.36 = f32[3072,768]{1,0:T(8,128)} fusion(f32[192,768]{1,0:T(8,128)} %param.28, f32[192,3072]{1,0:T(8,128)S(1)} %copy-done.3), kind=kOutput, calls=%fused_computation.65 | convolution fusion | flops 5440536576 | bytes 12386304 | tf_op jit(solution)/shard_map/dot_general | solution.py:32
  589.5 25.1 %reduce-scatter.10.cloned.1.call-done = f32[96,768]{1,0:T(8,128)} async-done(((f32[768,768]{1,0:T(8,128)}), f32[96,768]{1,0:T(8,128)}) %reduce-scatter.10.cloned.1.call-update) | async-done | bytes 294928 | tf_op jit(solution)/shard_map/reduce_scatter | solution.py:263
  614.6 46.2 %reduce-scatter.14.cloned.1.call-done = f32[96,768]{1,0:T(8,128)} async-done(((f32[768,768]{1,0:T(8,128)}), f32[96,768]{1,0:T(8,128)}) %reduce-scatter.14.cloned.1.call-update) | async-done | bytes 294928 | tf_op jit(solution)/shard_map/reduce_scatter | solution.py:266
  660.8 45.7 %reduce-scatter.12.cloned.1.call-done = f32[96,768]{1,0:T(8,128)} async-done(((f32[768,768]{1,0:T(8,128)}), f32[96,768]{1,0:T(8,128)}) %reduce-scatter.12.cloned.1.call-update) | async-done | bytes 294928 | tf_op jit(solution)/shard_map/reduce_scatter | solution.py:265
  706.5 80.4 %reduce-scatter.18.cloned.1.call-done = f32[96,3072]{1,0:T(8,128)} async-done(((f32[768,3072]{1,0:T(8,128)}), f32[96,3072]{1,0:T(8,128)}) %reduce-scatter.18.cloned.1.call-update) | async-done | bytes 1179664 | tf_op jit(solution)/shard_map/reduce_scatter | solution.py:270
  787.0 80.3 %reduce-scatter.20.cloned.1.call-done = f32[384,768]{1,0:T(8,128)} async-done(((f32[3072,768]{1,0:T(8,128)}), f32[384,768]{1,0:T(8,128)}) %reduce-scatter.20.cloned.1.call-update) | async-done | bytes 1179664 | tf_op jit(solution)/shard_map/reduce_scatter | solution.py:272
  872.6 5.2 fusion.77
  879.8 4.5 convolution_add_fusion.2
  888.4 26.3 %all-reduce.17 = (f32[768]{0:T(1024)}, f32[768]{0:T(1024)}, f32[768]{0:T(1024)}, f32[768]{0:T(1024)}, f32[3072]{0:T(1024)}, /*index=5*/f32[768]{0:T(1024)}, f32[...) all-reduce(f32[768]{0:T(1024)} %dynamic-update-slice.7, ...), channel_id=1, replica_groups=mesh['dp'=4,'blk'=2,'ulys'=4] {'blk','ulys'}, use_global_device_ids=true, to_apply=%add.7 | all-reduce | flops 9984 | bytes 79872
  926.1 13.0 %all-reduce.19 = (f32[96]{0:T(128)}, f32[96]{0:T(128)}, f32[96]{0:T(128)}, f32[384]{0:T(512)}, f32[96]{0:T(128)}, /*index=5*/f32[96]{0:T(128)}, f32[96]{0:T(128)}, f32[96]{0:T(128)}, f32[96]{0:T(128)}) all-reduce(f32[96]{0:T(128)} %dynamic-slice.9, f32[96]{0:T(128)} %dynamic-slice.11, ...), channel_id=1, replica_groups=mesh['dp'=4,'blk'=2,'ulys'=4] {'dp'}, use_global_device_ids=true, to_apply=%region_20.21 | all-reduce | flops 1152 | bytes 9216 | tf_op jit(solution)/shard_map/psum | solution.py:279
  943.3 10.4 %fusion.35 = f32[192,768]{1,0:T(8,128)} fusion(f32[192,768]{1,0:T(8,128)S(1)} %copy-done.6, f32[3072,768]{1,0:T(8,128)} %all-gather.22.cloned.1.call-done, f32[192,3072]{1,0:T(8,128)S(1)} %copy-done.3, f32[768]{0:T(1024)S(1)} %copy-done.51), kind=kOutput, calls=%fused_computation.63 | convolution fusion | flops 5440831488 | bytes 12979200 | tf_op jit(solution)/shard_map/dot_general | solution.py:28
  953.6 52.7 %all-reduce.23.cloned.1.call-done = (f32[96,768]{1,0:T(8,128)}, f32[96,768]{1,0:T(8,128)}, f32[96,768]{1,0:T(8,128)}, f32[96,768]{1,0:T(8,128)}, f32[96,3072]{1,0:T(8,128)}, /*index=5*/f32[384,768]{1,0:T(8,128)}) async-done(((f32[96,768]{1,0:T(8,128)}, f32[96,768]{1,0:T(8,128)}, f32[96,768]{1,0:T(8,128)}, f32[96,768]{1,0:T(8,128)}, f32[96,3072]{1,0:T(8,128)}, /*index=5*/f32[384,768]{1,0:T(8,128)}), ...) | async-done | bytes 3538960 | tf_op jit(solution)/shard_map/psum | solution.py:279
  (318 shorter events, 168.2 us)
Async XLA Ops:
  7.2 39.7 %copy-start = (f32[192,768]{1,0:T(8,128)S(1)}, f32[192,768]{1,0:T(8,128)}, u32[]{:S(2)}) copy-start(f32[192,768]{1,0:T(8,128)} %param.24) | copy-start | bytes 1769476
  7.2 39.7 %all-gather.12.cloned.1.call-start = ((), (), s32[]{:S(2)}) async-start(), calls=%async_computation.16 | async-start | bytes 2654208 | tf_op jit(solution)/shard_map/all_gather | solution.py:81
  7.9 66.7 %all-gather.10.cloned.1.call-start = ((), (), s32[]{:S(2)}) async-start(), calls=%async_computation.15 | async-start | bytes 2654208 | tf_op jit(solution)/shard_map/all_gather | solution.py:80
  8.7 99.4 %all-gather.16.cloned.1.call-start = ((), (), s32[]{:S(2)}) async-start(), calls=%async_computation.18 | async-start | bytes 2654208 | tf_op jit(solution)/shard_map/all_gather | solution.py:78
  44.4 30.3 %copy-start.31 = (f32[768]{0:T(1024)}, f32[768]{0:T(1024)S(1)}, u32[]{:S(2)}) copy-start(f32[768]{0:T(1024)S(1)} %get-tuple-element.345) | copy-start | bytes 9220
  44.4 30.3 %copy-start.37 = (f32[768]{0:T(1024)}, f32[768]{0:T(1024)S(1)}, u32[]{:S(2)}) copy-start(f32[768]{0:T(1024)S(1)} %get-tuple-element.344) | copy-start | bytes 9220
  45.6 29.1 %copy-start.42 = (f32[192]{0:T(256)}, f32[192]{0:T(256)S(1)}, u32[]{:S(2)}) copy-start(f32[192]{0:T(256)S(1)} %broadcast_multiply_fusion.1) | copy-start | bytes 2308
  46.9 27.8 %copy-start.47 = (f32[192]{0:T(256)}, f32[192]{0:T(256)S(1)}, u32[]{:S(2)}) copy-start(f32[192]{0:T(256)S(1)} %fusion.49) | copy-start | bytes 2308
  51.6 29.5 %all-to-all-start.1 = ((f32[192,4,192]{0,2,1:T(8,128)}), f32[192,4,192]{0,2,1:T(8,128)S(1)}, u32[]{:S(2)}, u32[]{:S(2)}) async-start(f32[192,4,192]{0,2,1:T(8,128)} %bitcast.3), calls=%async_computation.1 | async-start | bytes 1572864 | tf_op jit(solution)/shard_map/all_to_all | solution.py:104
  81.1 16.7 %all-to-all-start = ((f32[192,4,192]{0,2,1:T(8,128)}), f32[192,4,192]{0,2,1:T(8,128)S(1)}, u32[]{:S(2)}, u32[]{:S(2)}) async-start(f32[192,4,192]{0,2,1:T(8,128)} %bitcast.1), calls=%async_computation | async-start | bytes 1572864 | tf_op jit(solution)/shard_map/all_to_all | solution.py:103
  84.6 61.6 %all-gather.14.cloned.1.call-start = ((), (), s32[]{:S(2)}) async-start(), calls=%async_computation.17 | async-start | bytes 3538944 | tf_op jit(solution)/shard_map/all_gather | solution.py:167
  99.9 8.2 copy-start.38
  99.9 8.2 copy-start.43
  99.9 8.2 copy-start.48
  99.9 8.2 copy-start.57
  99.9 129.6 %all-gather.18.cloned.1.call-start = ((), (), s32[]{:S(2)}) async-start(), calls=%async_computation.19 | async-start | bytes 2654208 | tf_op jit(solution)/shard_map/all_gather | solution.py:83
  100.5 144.4 %all-gather.20.cloned.1.call-start = ((), (), s32[]{:S(2)}) async-start(), calls=%async_computation.20 | async-start | bytes 10616832 | tf_op jit(solution)/shard_map/all_gather | solution.py:85
  101.1 203.6 %all-gather.22.cloned.1.call-start = ((), (), s32[]{:S(2)}) async-start(), calls=%async_computation.21 | async-start | bytes 10616832 | tf_op jit(solution)/shard_map/all_gather | solution.py:87
  113.2 15.2 %all-to-all-start.2 = ((f32[192,4,192]{2,0,1:T(8,128)}), f32[192,4,192]{2,0,1:T(8,128)S(1)}, u32[]{:S(2)}, u32[]{:S(2)}) async-start(f32[192,4,192]{2,0,1:T(8,128)} %copy.98), calls=%async_computation.2 | async-start | bytes 1572864 | tf_op jit(solution)/shard_map/all_to_all | solution.py:102
  200.2 28.3 %copy-start.19 = (f32[768,192]{0,1:T(8,128)}, f32[768,192]{0,1:T(8,128)S(1)}, u32[]{:S(2)}) copy-start(f32[768,192]{0,1:T(8,128)S(1)} %get-tuple-element.134) | copy-start | bytes 1769476
  202.2 27.3 %copy-start.56 = (f32[768]{0:T(1024)S(1)}, f32[768]{0:T(1024)}, u32[]{:S(2)}) copy-start(f32[768]{0:T(1024)} %get-tuple-element.347) | copy-start | bytes 9220
  202.2 26.3 %all-to-all-start.3 = ((f32[4,192,192]{2,1,0:T(8,128)}), f32[4,192,192]{2,1,0:T(8,128)S(1)}, u32[]{:S(2)}, u32[]{:S(2)}) async-start(f32[4,192,192]{2,1,0:T(8,128)} %bitcast.9), calls=%async_computation.3 | async-start | bytes 1572864 | tf_op jit(solution)/shard_map/all_to_all | solution.py:176
  233.3 11.6 %copy-start.40 = (f32[192]{0:T(256)}, f32[192]{0:T(256)S(1)}, u32[]{:S(2)}) copy-start(f32[192]{0:T(256)S(1)} %broadcast_multiply_fusion) | copy-start | bytes 2308
  234.3 10.6 %copy-start.54 = (f32[192]{0:T(256)}, f32[192]{0:T(256)S(1)}, u32[]{:S(2)}) copy-start(f32[192]{0:T(256)S(1)} %multiply_reduce_fusion.5) | copy-start | bytes 2308
  253.9 65.2 %copy-start.2 = (f32[192,3072]{1,0:T(8,128)}, f32[192,3072]{1,0:T(8,128)S(1)}, u32[]{:S(2)}) copy-start(f32[192,3072]{1,0:T(8,128)S(1)} %convolution_add_fusion) | copy-start | bytes 7077892
  304.7 14.4 %copy-start.5 = (f32[192,768]{1,0:T(8,128)S(1)}, f32[192,768]{1,0:T(8,128)}, u32[]{:S(2)}) copy-start(f32[192,768]{1,0:T(8,128)} %copy-done.4) | copy-start | bytes 1769476
  304.7 14.4 %copy-start.7 = (f32[768,3072]{1,0:T(8,128)S(1)}, f32[768,3072]{1,0:T(8,128)}, u32[]{:S(2)}) copy-start(f32[768,3072]{1,0:T(8,128)} %all-gather.20.cloned.1.call-done) | copy-start | bytes 28311556
  304.7 14.4 %copy-start.34 = (f32[768]{0:T(1024)S(1)}, f32[768]{0:T(1024)}, u32[]{:S(2)}) copy-start(f32[768]{0:T(1024)} %get-tuple-element.349) | copy-start | bytes 9220
  304.7 14.4 %copy-start.41 = (f32[192]{0:T(256)S(1)}, f32[192]{0:T(256)}, u32[]{:S(2)}) copy-start(f32[192]{0:T(256)} %copy-done.40) | copy-start | bytes 2308
  304.7 14.4 %copy-start.46 = (f32[192]{0:T(256)S(1)}, f32[192]{0:T(256)}, u32[]{:S(2)}) copy-start(f32[192]{0:T(256)} %fusion.50) | copy-start | bytes 2308
  319.1 10.2 copy-start.12
  319.2 10.2 copy-start.55
  319.2 10.5 %copy-start.24 = (f32[192,768]{1,0:T(8,128)S(1)}, f32[192,768]{1,0:T(8,128)}, u32[]{:S(2)}) copy-start(f32[192,768]{1,0:T(8,128)} %param.28) | copy-start | bytes 1769476
  335.4 20.0 %copy-start.20 = (f32[768,192]{0,1:T(8,128)S(1)}, f32[768,192]{0,1:T(8,128)}, u32[]{:S(2)}) copy-start(f32[768,192]{0,1:T(8,128)} %copy-done.19) | copy-start | bytes 1769476
  335.4 16.1 %all-to-all-start.4 = ((f32[192,4,192]{2,0,1:T(8,128)}), f32[192,4,192]{2,0,1:T(8,128)}, u32[]{:S(2)}, u32[]{:S(2)}) async-start(f32[192,4,192]{2,0,1:T(8,128)} %copy.103), calls=%async_computation.4 | async-start | bytes 1572864 | tf_op jit(solution)/shard_map/all_to_all | solution.py:202
  339.7 176.8 %reduce-scatter.8.cloned.1.call-start = ((), (), s32[]{:S(2)}) async-start(), calls=%async_computation.22 | async-start | bytes 3538944 | tf_op jit(solution)/shard_map/reduce_scatter | solution.py:242
  481.6 107.9 %reduce-scatter.16.cloned.1.call-start = ((), (), s32[]{:S(2)}) async-start(), calls=%async_computation.26 | async-start | bytes 2654208 | tf_op jit(solution)/shard_map/reduce_scatter | solution.py:268
  486.4 128.2 %reduce-scatter.10.cloned.1.call-start = ((), (), s32[]{:S(2)}) async-start(), calls=%async_computation.23 | async-start | bytes 2654208 | tf_op jit(solution)/shard_map/reduce_scatter | solution.py:263
  486.7 16.0 %copy-start.33 = (f32[768]{0:T(1024)S(1)}, f32[768]{0:T(1024)}, u32[]{:S(2)}) copy-start(f32[768]{0:T(1024)} %copy-done.31) | copy-start | bytes 9220
  486.7 16.0 %copy-start.39 = (f32[768]{0:T(1024)S(1)}, f32[768]{0:T(1024)}, u32[]{:S(2)}) copy-start(f32[768]{0:T(1024)} %copy-done.37) | copy-start | bytes 9220
  486.7 16.0 %copy-start.44 = (f32[192]{0:T(256)S(1)}, f32[192]{0:T(256)}, u32[]{:S(2)}) copy-start(f32[192]{0:T(256)} %copy-done.42) | copy-start | bytes 2308
  486.8 16.0 %copy-start.49 = (f32[192]{0:T(256)S(1)}, f32[192]{0:T(256)}, u32[]{:S(2)}) copy-start(f32[192]{0:T(256)} %copy-done.47) | copy-start | bytes 2308
  506.4 154.4 %reduce-scatter.14.cloned.1.call-start = ((), (), s32[]{:S(2)}) async-start(), calls=%async_computation.25 | async-start | bytes 2654208 | tf_op jit(solution)/shard_map/reduce_scatter | solution.py:266
  537.8 168.7 %reduce-scatter.12.cloned.1.call-start = ((), (), s32[]{:S(2)}) async-start(), calls=%async_computation.24 | async-start | bytes 2654208 | tf_op jit(solution)/shard_map/reduce_scatter | solution.py:265
  565.0 222.0 %reduce-scatter.18.cloned.1.call-start = ((), (), s32[]{:S(2)}) async-start(), calls=%async_computation.27 | async-start | bytes 10616832 | tf_op jit(solution)/shard_map/reduce_scatter | solution.py:270
  576.0 291.3 %reduce-scatter.20.cloned.1.call-start = ((), (), s32[]{:S(2)}) async-start(), calls=%async_computation.28 | async-start | bytes 10616832 | tf_op jit(solution)/shard_map/reduce_scatter | solution.py:272
  589.4 279.8 %copy-start.60 = (f32[96]{0:T(128)S(1)}, f32[96]{0:T(128)}, u32[]{:S(2)}) copy-start(f32[96]{0:T(128)} %param.39) | copy-start | bytes 1156
  589.4 416.9 %all-reduce.23.cloned.1.call-start = ((), (), s32[]{:S(2)}) async-start(), calls=%async_computation.29 | async-start | bytes 7077888 | tf_op jit(solution)/shard_map/psum | solution.py:279
  (39 other events, 163.4 us)
Sparse Core Ops, SparseCore 0:
  9.9 32.0 all-gather.11
  43.9 30.6 all-gather.9
  76.5 31.5 all-gather.15
  110.1 36.0 all-gather.13
  147.9 29.0 all-gather.17
  178.8 66.0 all-gather.19
  246.8 57.9 all-gather.21
  481.7 34.7 reduce-scatter.7
  520.2 48.6 reduce-scatter.15
  572.1 42.4 reduce-scatter.9
  618.3 42.4 reduce-scatter.13
  664.0 42.4 reduce-scatter.11
  710.4 76.4 reduce-scatter.17
  790.7 76.4 reduce-scatter.19
  870.2 136.1 all-reduce.22
where the time goes:
time: 1030 us; the launch traced here: 1020 us
  waiting for transfers between devices  476 us (46%)
  matrix products  211 us (20%)
  blocking collectives  141 us (14%)
  local copies, waits for them, and re-layouts  91.2 us (9%)
  loops' own time  40.3 us (4%)
  other arithmetic  25.8 us (3%)
  starting transfers between devices  19.3 us (2%)
  between operations  17.2 us (2%)
    reduce_scatter x1, waiting for transfers between devices, local(): lax.psum_scatter(grad_upproj, ('blk', 'ulys'), scatter_dimension=0, tiled...  80.4 us
    reduce_scatter x1, waiting for transfers between devices, local(): lax.psum_scatter(grad_downproj, ('blk', 'ulys'), scatter_dimension=0, til...  80.3 us
    psum x1, waiting for transfers between devices, local(): lax.psum((shard_sums[0], shard_sums[1], shard_sums[2], shard_sums[3], sha...  52.7 us
    unnamed x2, blocking collectives  52.7 us
    all_gather x1, waiting for transfers between devices, local(): lax.all_gather(w_down, ('blk', 'ulys'), axis=0, tiled=True)  50.8 us
    reduce_scatter x1, waiting for transfers between devices, local(): lax.psum_scatter(grad_value, ('blk', 'ulys'), scatter_dimension=0, tiled=...  46.2 us
    reduce_scatter x1, waiting for transfers between devices, local(): lax.psum_scatter(grad_key, ('blk', 'ulys'), scatter_dimension=0, tiled=True)  45.7 us
    dot_general x6, matrix products, matmul_right_t(): lax.dot_general(left, right, (((1,), (1,)), ((), ())), precision=HIGH)  40.7 us
  transfers between devices with their start and end apart: 20, of which 15 were waited for; matrix products, arithmetic and copies ran while one was open for 18% of the time, Pallas kernels for 0%

commit v1 on v0

--- a/solution.py
+++ b/solution.py
@@ -242,7 +242,15 @@
     local_pairs = lax.psum_scatter(pair_grads, "blk", scatter_dimension=0, tiled=True)
     token_query_grad, token_keys_grad, token_values_grad = (
         lax.all_to_all(query_grad, "ulys", split_axis=0, concat_axis=1, tiled=True),
-        lax.all_to_all(local_pairs[:, :width], "ulys", split_axis=0, concat_axis=1, tiled=True),
+        jnp.concatenate(
+            lax.all_to_all(
+                jnp.stack(jnp.split(local_pairs[:, :width], lax.axis_size("ulys"), axis=0)),
+                "ulys",
+                0,
+                0,
+            ),
+            axis=1,
+        ),
         lax.all_to_all(local_pairs[:, width:], "ulys", split_axis=0, concat_axis=1, tiled=True),
     )
     grad_query = matmul_left_t(normalized_rows, token_query_grad)

time: 1030 us -> 1030 us (level)
    unnamed x152 -> x154, local copies, waits for them, and re-layouts: 38.2 us -> 39.1 us
where the time goes in v1:
time: 1030 us; the launch traced here: 1020 us
  waiting for transfers between devices  476 us (46%)
  matrix products  212 us (21%)
  blocking collectives  139 us (13%)
  local copies, waits for them, and re-layouts  91.3 us (9%)
  loops' own time  40.6 us (4%)
  other arithmetic  26.4 us (3%)
  starting transfers between devices  19.3 us (2%)
  between operations  17.2 us (2%)
    reduce_scatter x1, waiting for transfers between devices, local(): lax.psum_scatter(grad_upproj, ('blk', 'ulys'), scatter_dimension=0, tiled...  80.4 us
    reduce_scatter x1, waiting for transfers between devices, local(): lax.psum_scatter(grad_downproj, ('blk', 'ulys'), scatter_dimension=0, til...  80.3 us
    psum x1, waiting for transfers between devices, local(): lax.psum((shard_sums[0], shard_sums[1], shard_sums[2], shard_sums[3], sha...  53.8 us
    unnamed x2, blocking collectives  52.1 us
    all_gather x1, waiting for transfers between devices, local(): lax.all_gather(w_down, ('blk', 'ulys'), axis=0, tiled=True)  50.8 us
    reduce_scatter x1, waiting for transfers between devices, local(): lax.psum_scatter(grad_key, ('blk', 'ulys'), scatter_dimension=0, tiled=True)  46.3 us
    reduce_scatter x1, waiting for transfers between devices, local(): lax.psum_scatter(grad_value, ('blk', 'ulys'), scatter_dimension=0, tiled=...  45.7 us
    another operation x2, loops' own time, over_blocks(): state, unused = lax.scan(visit, state, (kv_blocks, code_blocks, offsets))  40.6 us
  transfers between devices with their start and end apart: 20, of which 15 were waited for; matrix products, arithmetic and copies ran while one was open for 18% of the time, Pallas kernels for 0%

profile of v1, /device:TPU:0, one launch (start us, length us, event | category | flops | bytes accessed | tf_op | source)
XLA Modules:
  0.0 1022.2 jit_solution(16879930637412951040)
XLA Ops:
  18.0 26.4 %all-reduce.18 = (f32[768]{0:T(1024)S(1)}, f32[768]{0:T(1024)S(1)}, f32[768]{0:T(1024)S(1)}, f32[768]{0:T(1024)}, f32[768]{0:T(1024)}, /*index=5*/f32[768]{0:T(1024)}, f32[768]{0:T(1024)}) all-reduce(f32[768]{0:T(1024)S(1)} %dynamic-update-slice.2, ...), channel_id=1, replica_groups=mesh['dp'=4,'blk'=2,'ulys'=4] {'blk','ulys'}, use_global_device_ids=true, to_apply=%add.2 | all-reduce | flops 5376 | bytes 43008
  55.1 19.6 %all-gather.10.cloned.1.call-done = f32[768,768]{1,0:T(8,128)} async-done(((f32[96,768]{1,0:T(8,128)}), f32[768,768]{1,0:T(8,128)}) %all-gather.10.cloned.1.call-update) | async-done | bytes 2359312 | tf_op jit(solution)/shard_map/all_gather | solution.py:80
  74.7 6.5 fusion.62
  85.7 12.1 %all-to-all-done = f32[192,4,192]{0,2,1:T(8,128)S(1)} async-done(((f32[192,4,192]{0,2,1:T(8,128)}), f32[192,4,192]{0,2,1:T(8,128)S(1)}, u32[]{:S(2)}, u32[]{:S(2)}) %all-to-all-start) | async-done | bytes 589856 | tf_op jit(solution)/shard_map/all_to_all | solution.py:103
  101.9 6.2 all-gather.16.cloned.1.call-done
  122.9 5.5 all-to-all-done.2
  129.3 16.9 %all-gather.14.cloned.1.call-done = f32[1536,384]{0,1:T(8,128)} async-done(((f32[768,384]{0,1:T(8,128)}), f32[1536,384]{0,1:T(8,128)}) %all-gather.14.cloned.1.call-update) | async-done | bytes 2359312 | tf_op jit(solution)/shard_map/all_gather | solution.py:167
  150.3 49.9 %while.28 = (s32[]{:T(128)}, f32[3,768]{1,0:T(4,128)S(1)}, f32[3,768]{1,0:T(4,128)}, f32[768,192]{0,1:T(8,128)S(1)}, f32[768]{0:T(1024)}, /*index=5*/f32[2,768]{...) while((s32[]{:T(128)}, f32[3,768]{1,0:T(4,128)S(1)}, ...), condition=%wide.region_5.6_spmd.clone, body=%wide.region_2.5_spmd.clone.sunk | while | flops 2741222400 | bytes 31506652 | solution.py:144
  155.6 6.9 fusion.145
  162.5 6.2 fusion.149
  176.3 6.9 fusion.145
  183.3 6.2 fusion.149
  205.9 22.2 %all-gather.1 = f32[8,1,384]{2,1,0:T(1,128)} all-gather(f32[1,1,384]{2,1,0:T(1,128)S(1)} %reshape.342), channel_id=1, replica_groups=mesh['dp'=4,'blk'=2,'ulys'=4] {'blk','ulys'}, dimensions={0}, use_global_device_ids=true | all-gather | bytes 13824 | tf_op jit(solution)/shard_map/all_gather | solution.py:86
  234.5 10.4 %all-gather.20.cloned.1.call-done = f32[768,3072]{1,0:T(8,128)} async-done(((f32[96,3072]{1,0:T(8,128)}), f32[768,3072]{1,0:T(8,128)}) %all-gather.20.cloned.1.call-update) | async-done | bytes 9437200 | tf_op jit(solution)/shard_map/all_gather | solution.py:85
  244.9 9.0 convolution_add_fusion
  253.9 50.8 %all-gather.22.cloned.1.call-done = f32[3072,768]{1,0:T(8,128)} async-done(((f32[384,768]{1,0:T(8,128)}), f32[3072,768]{1,0:T(8,128)}) %all-gather.22.cloned.1.call-update) | async-done | bytes 9437200 | tf_op jit(solution)/shard_map/all_gather | solution.py:87
  304.7 14.4 %fusion.64 = (f32[3072]{0:T(1024)}, f32[192,3072]{1,0:T(8,128)S(1)}) fusion(f32[192,3072]{1,0:T(8,128)S(1)} %convolution_add_fusion, f32[192,768]{1,0:T(8,128)} %param.28, f32[3072,768]{1,0:T(8,128)} %all-gather.22.cloned.1.call-done), kind=kOutput, calls=%fused_computation.128 | convolution fusion | flops 5449970688 | bytes 14757888 | tf_op jit(solution)/shard_map/dot_general | solution.py:36
  319.2 10.1 multiply_reduce_fusion
  340.4 11.0 %all-to-all-done.4 = f32[192,4,192]{2,0,1:T(8,128)} async-done(((f32[192,4,192]{2,0,1:T(8,128)}), f32[192,4,192]{2,0,1:T(8,128)}, u32[]{:S(2)}, u32[]{:S(2)}) %all-to-all-start.4) | async-done | bytes 589856 | tf_op jit(solution)/shard_map/all_to_all | solution.py:202
  357.7 124.2 %while.29 = (s32[]{:T(128)}, f32[768,192]{0,1:T(8,128)S(1)}, f32[1536,384]{0,1:T(8,128)}, f32[2,768,384]{1,2,0:T(8,128)}, f32[768]{0:T(1024)S(1)}, /*index=5*/f3...) while((s32[]{:T(128)}, f32[768,192]{0,1:T(8,128)S(1)}, ...), condition=%wide.region_12.13_spmd.clone, body=%wide.region_11.12_spmd.clone.sunk | while | flops 6813353472 | bytes 72011080 | solution.py:144
  384.5 6.0 fusion.161
  390.5 8.8 fusion.164
  399.4 8.7 fusion.162
  412.3 6.9 fusion.165
  419.8 6.9 dynamic_update_slice.5
  433.0 6.0 fusion.161
  439.0 8.8 fusion.164
  447.8 8.7 fusion.162
  460.8 6.9 fusion.165
  468.3 6.1 dynamic_update_slice.5
  487.1 14.1 %all_to_all.132 = f32[4,192,192]{2,1,0:T(8,128)S(1)} all-to-all(f32[4,192,192]{2,1,0:T(8,128)S(1)} %bitcast.220), channel_id=1, replica_groups=mesh['dp'=4,'blk'=2,'ulys'=4] {'ulys'}, dimensions={0} | all-to-all | bytes 1179648 | tf_op jit(solution)/shard_map/all_to_all | solution.py:244
  506.9 10.0 reduce-scatter.8.cloned.1.call-done
  518.4 14.2 %all_to_all.133 = f32[4,192,192]{1,2,0:T(8,128)S(1)} all-to-all(f32[4,192,192]{1,2,0:T(8,128)S(1)} %pad_maximum_fusion.1), channel_id=1, replica_groups=mesh['dp'=4,'blk'=2,'ulys'=4] {'ulys'}, dimensions={0} | all-to-all | bytes 1179648 | tf_op jit(solution)/shard_map/all_to_all | solution.py:246
  533.4 5.4 fusion.60
  540.2 18.5 %all_to_all.134 = f32[4,192,192]{2,1,0:T(8,128)S(1)} all-to-all(f32[4,192,192]{2,1,0:T(8,128)S(1)} %bitcast.221), channel_id=1, replica_groups=mesh['dp'=4,'blk'=2,'ulys'=4] {'ulys'}, dimensions={0} | all-to-all | bytes 1179648 | tf_op jit(solution)/shard_map/all_to_all | solution.py:254
  561.4 4.9 fusion.59
  566.4 11.0 %fusion.37 = f32[768,3072]{1,0:T(8,128)} fusion(f32[192,3072]{1,0:T(8,128)S(1)} %copy-done.14, f32[192,768]{1,0:T(8,128)S(1)} %copy-done.6, f32[768]{0:T(1024)S(1)} %copy-done.37, f32[768]{0:T(1024)S(1)} %copy-done.36, f32[192]{0:T(256)} %fusion.50, f32[192]{0:T(256)} %copy-done.41), kind=kOutput, calls=%fused_computation.83 | convolution fusion | flops 5436407808 | bytes 12393984 | tf_op jit(solution)/shard_map/dot_general | solution.py:32
  579.1 11.7 %fusion.36 = f32[3072,768]{1,0:T(8,128)} fusion(f32[192,768]{1,0:T(8,128)} %param.28, f32[192,3072]{1,0:T(8,128)S(1)} %copy-done.3), kind=kOutput, calls=%fused_computation.65 | convolution fusion | flops 5440536576 | bytes 12386304 | tf_op jit(solution)/shard_map/dot_general | solution.py:32
  590.9 23.7 %reduce-scatter.10.cloned.1.call-done = f32[96,768]{1,0:T(8,128)} async-done(((f32[768,768]{1,0:T(8,128)}), f32[96,768]{1,0:T(8,128)}) %reduce-scatter.10.cloned.1.call-update) | async-done | bytes 294928 | tf_op jit(solution)/shard_map/reduce_scatter | solution.py:271
  614.6 46.3 %reduce-scatter.12.cloned.1.call-done = f32[96,768]{1,0:T(8,128)} async-done(((f32[768,768]{1,0:T(8,128)}), f32[96,768]{1,0:T(8,128)}) %reduce-scatter.12.cloned.1.call-update) | async-done | bytes 294928 | tf_op jit(solution)/shard_map/reduce_scatter | solution.py:273
  660.8 45.7 %reduce-scatter.14.cloned.1.call-done = f32[96,768]{1,0:T(8,128)} async-done(((f32[768,768]{1,0:T(8,128)}), f32[96,768]{1,0:T(8,128)}) %reduce-scatter.14.cloned.1.call-update) | async-done | bytes 294928 | tf_op jit(solution)/shard_map/reduce_scatter | solution.py:274
  706.6 80.4 %reduce-scatter.18.cloned.1.call-done = f32[96,3072]{1,0:T(8,128)} async-done(((f32[768,3072]{1,0:T(8,128)}), f32[96,3072]{1,0:T(8,128)}) %reduce-scatter.18.cloned.1.call-update) | async-done | bytes 1179664 | tf_op jit(solution)/shard_map/reduce_scatter | solution.py:278
  787.0 80.3 %reduce-scatter.20.cloned.1.call-done = f32[384,768]{1,0:T(8,128)} async-done(((f32[3072,768]{1,0:T(8,128)}), f32[384,768]{1,0:T(8,128)}) %reduce-scatter.20.cloned.1.call-update) | async-done | bytes 1179664 | tf_op jit(solution)/shard_map/reduce_scatter | solution.py:280
  874.5 6.6 fusion.76
  887.7 25.7 %all-reduce.17 = (f32[768]{0:T(1024)}, f32[768]{0:T(1024)}, f32[768]{0:T(1024)}, f32[768]{0:T(1024)}, f32[3072]{0:T(1024)}, /*index=5*/f32[768]{0:T(1024)}, f32[...) all-reduce(f32[768]{0:T(1024)} %dynamic-update-slice.7, ...), channel_id=1, replica_groups=mesh['dp'=4,'blk'=2,'ulys'=4] {'blk','ulys'}, use_global_device_ids=true, to_apply=%add.7 | all-reduce | flops 9984 | bytes 79872
  924.8 13.3 %all-reduce.19 = (f32[96]{0:T(128)}, f32[96]{0:T(128)}, f32[96]{0:T(128)}, f32[384]{0:T(512)}, f32[96]{0:T(128)}, /*index=5*/f32[96]{0:T(128)}, f32[96]{0:T(128)}, f32[96]{0:T(128)}, f32[96]{0:T(128)}) all-reduce(f32[96]{0:T(128)} %dynamic-slice.9, f32[96]{0:T(128)} %dynamic-slice.11, ...), channel_id=1, replica_groups=mesh['dp'=4,'blk'=2,'ulys'=4] {'dp'}, use_global_device_ids=true, to_apply=%region_20.21 | all-reduce | flops 1152 | bytes 9216 | tf_op jit(solution)/shard_map/psum | solution.py:287
  942.2 10.3 %fusion.35 = f32[192,768]{1,0:T(8,128)} fusion(f32[192,768]{1,0:T(8,128)S(1)} %copy-done.6, f32[3072,768]{1,0:T(8,128)} %all-gather.22.cloned.1.call-done, f32[192,3072]{1,0:T(8,128)S(1)} %copy-done.3, f32[768]{0:T(1024)S(1)} %copy-done.52), kind=kOutput, calls=%fused_computation.63 | convolution fusion | flops 5440831488 | bytes 12979200 | tf_op jit(solution)/shard_map/dot_general | solution.py:28
  952.5 53.8 %all-reduce.23.cloned.1.call-done = (f32[96,768]{1,0:T(8,128)}, f32[96,768]{1,0:T(8,128)}, f32[96,768]{1,0:T(8,128)}, f32[96,768]{1,0:T(8,128)}, f32[96,3072]{1,0:T(8,128)}, /*index=5*/f32[384,768]{1,0:T(8,128)}) async-done(((f32[96,768]{1,0:T(8,128)}, f32[96,768]{1,0:T(8,128)}, f32[96,768]{1,0:T(8,128)}, f32[96,768]{1,0:T(8,128)}, f32[96,3072]{1,0:T(8,128)}, /*index=5*/f32[384,768]{1,0:T(8,128)}), ...) | async-done | bytes 3538960 | tf_op jit(solution)/shard_map/psum | solution.py:287
  (320 shorter events, 167.6 us)
Async XLA Ops:
  7.2 39.7 %copy-start = (f32[192,768]{1,0:T(8,128)S(1)}, f32[192,768]{1,0:T(8,128)}, u32[]{:S(2)}) copy-start(f32[192,768]{1,0:T(8,128)} %param.24) | copy-start | bytes 1769476
  7.2 39.7 %all-gather.12.cloned.1.call-start = ((), (), s32[]{:S(2)}) async-start(), calls=%async_computation.16 | async-start | bytes 2654208 | tf_op jit(solution)/shard_map/all_gather | solution.py:81
  7.9 66.7 %all-gather.10.cloned.1.call-start = ((), (), s32[]{:S(2)}) async-start(), calls=%async_computation.15 | async-start | bytes 2654208 | tf_op jit(solution)/shard_map/all_gather | solution.py:80
  8.7 99.4 %all-gather.16.cloned.1.call-start = ((), (), s32[]{:S(2)}) async-start(), calls=%async_computation.18 | async-start | bytes 2654208 | tf_op jit(solution)/shard_map/all_gather | solution.py:78
  44.4 30.3 %copy-start.32 = (f32[768]{0:T(1024)}, f32[768]{0:T(1024)S(1)}, u32[]{:S(2)}) copy-start(f32[768]{0:T(1024)S(1)} %get-tuple-element.345) | copy-start | bytes 9220
  44.4 30.3 %copy-start.38 = (f32[768]{0:T(1024)}, f32[768]{0:T(1024)S(1)}, u32[]{:S(2)}) copy-start(f32[768]{0:T(1024)S(1)} %get-tuple-element.344) | copy-start | bytes 9220
  45.6 29.1 %copy-start.43 = (f32[192]{0:T(256)}, f32[192]{0:T(256)S(1)}, u32[]{:S(2)}) copy-start(f32[192]{0:T(256)S(1)} %broadcast_multiply_fusion.1) | copy-start | bytes 2308
  46.9 27.8 %copy-start.48 = (f32[192]{0:T(256)}, f32[192]{0:T(256)S(1)}, u32[]{:S(2)}) copy-start(f32[192]{0:T(256)S(1)} %fusion.49) | copy-start | bytes 2308
  51.6 29.5 %all-to-all-start.1 = ((f32[192,4,192]{0,2,1:T(8,128)}), f32[192,4,192]{0,2,1:T(8,128)S(1)}, u32[]{:S(2)}, u32[]{:S(2)}) async-start(f32[192,4,192]{0,2,1:T(8,128)} %bitcast.3), calls=%async_computation.1 | async-start | bytes 1572864 | tf_op jit(solution)/shard_map/all_to_all | solution.py:104
  81.1 16.7 %all-to-all-start = ((f32[192,4,192]{0,2,1:T(8,128)}), f32[192,4,192]{0,2,1:T(8,128)S(1)}, u32[]{:S(2)}, u32[]{:S(2)}) async-start(f32[192,4,192]{0,2,1:T(8,128)} %bitcast.1), calls=%async_computation | async-start | bytes 1572864 | tf_op jit(solution)/shard_map/all_to_all | solution.py:103
  84.6 61.6 %all-gather.14.cloned.1.call-start = ((), (), s32[]{:S(2)}) async-start(), calls=%async_computation.17 | async-start | bytes 3538944 | tf_op jit(solution)/shard_map/all_gather | solution.py:167
  99.9 8.2 copy-start.39
  99.9 8.2 copy-start.44
  99.9 8.2 copy-start.49
  99.9 8.2 copy-start.58
  99.9 129.2 %all-gather.18.cloned.1.call-start = ((), (), s32[]{:S(2)}) async-start(), calls=%async_computation.19 | async-start | bytes 2654208 | tf_op jit(solution)/shard_map/all_gather | solution.py:83
  100.5 144.3 %all-gather.20.cloned.1.call-start = ((), (), s32[]{:S(2)}) async-start(), calls=%async_computation.20 | async-start | bytes 10616832 | tf_op jit(solution)/shard_map/all_gather | solution.py:85
  101.1 203.6 %all-gather.22.cloned.1.call-start = ((), (), s32[]{:S(2)}) async-start(), calls=%async_computation.21 | async-start | bytes 10616832 | tf_op jit(solution)/shard_map/all_gather | solution.py:87
  113.2 15.2 %all-to-all-start.2 = ((f32[192,4,192]{2,0,1:T(8,128)}), f32[192,4,192]{2,0,1:T(8,128)S(1)}, u32[]{:S(2)}, u32[]{:S(2)}) async-start(f32[192,4,192]{2,0,1:T(8,128)} %copy.95), calls=%async_computation.2 | async-start | bytes 1572864 | tf_op jit(solution)/shard_map/all_to_all | solution.py:102
  200.2 27.9 %copy-start.20 = (f32[768,192]{0,1:T(8,128)}, f32[768,192]{0,1:T(8,128)S(1)}, u32[]{:S(2)}) copy-start(f32[768,192]{0,1:T(8,128)S(1)} %get-tuple-element.134) | copy-start | bytes 1769476
  202.2 27.0 %copy-start.57 = (f32[768]{0:T(1024)S(1)}, f32[768]{0:T(1024)}, u32[]{:S(2)}) copy-start(f32[768]{0:T(1024)} %get-tuple-element.347) | copy-start | bytes 9220
  202.2 25.9 %all-to-all-start.3 = ((f32[4,192,192]{2,1,0:T(8,128)}), f32[4,192,192]{2,1,0:T(8,128)S(1)}, u32[]{:S(2)}, u32[]{:S(2)}) async-start(f32[4,192,192]{2,1,0:T(8,128)} %bitcast.9), calls=%async_computation.3 | async-start | bytes 1572864 | tf_op jit(solution)/shard_map/all_to_all | solution.py:176
  232.9 12.0 %copy-start.41 = (f32[192]{0:T(256)}, f32[192]{0:T(256)S(1)}, u32[]{:S(2)}) copy-start(f32[192]{0:T(256)S(1)} %broadcast_multiply_fusion) | copy-start | bytes 2308
  233.9 11.0 %copy-start.55 = (f32[192]{0:T(256)}, f32[192]{0:T(256)S(1)}, u32[]{:S(2)}) copy-start(f32[192]{0:T(256)S(1)} %multiply_reduce_fusion.5) | copy-start | bytes 2308
  253.9 65.2 %copy-start.2 = (f32[192,3072]{1,0:T(8,128)}, f32[192,3072]{1,0:T(8,128)S(1)}, u32[]{:S(2)}) copy-start(f32[192,3072]{1,0:T(8,128)S(1)} %convolution_add_fusion) | copy-start | bytes 7077892
  304.7 14.4 %copy-start.5 = (f32[192,768]{1,0:T(8,128)S(1)}, f32[192,768]{1,0:T(8,128)}, u32[]{:S(2)}) copy-start(f32[192,768]{1,0:T(8,128)} %copy-done.4) | copy-start | bytes 1769476
  304.7 14.4 %copy-start.7 = (f32[768,3072]{1,0:T(8,128)S(1)}, f32[768,3072]{1,0:T(8,128)}, u32[]{:S(2)}) copy-start(f32[768,3072]{1,0:T(8,128)} %all-gather.20.cloned.1.call-done) | copy-start | bytes 28311556
  304.7 14.4 %copy-start.35 = (f32[768]{0:T(1024)S(1)}, f32[768]{0:T(1024)}, u32[]{:S(2)}) copy-start(f32[768]{0:T(1024)} %get-tuple-element.349) | copy-start | bytes 9220
  304.7 14.4 %copy-start.42 = (f32[192]{0:T(256)S(1)}, f32[192]{0:T(256)}, u32[]{:S(2)}) copy-start(f32[192]{0:T(256)} %copy-done.41) | copy-start | bytes 2308
  304.7 14.4 %copy-start.47 = (f32[192]{0:T(256)S(1)}, f32[192]{0:T(256)}, u32[]{:S(2)}) copy-start(f32[192]{0:T(256)} %fusion.50) | copy-start | bytes 2308
  319.1 10.2 copy-start.13
  319.2 10.1 copy-start.56
  319.2 10.5 %copy-start.25 = (f32[192,768]{1,0:T(8,128)S(1)}, f32[192,768]{1,0:T(8,128)}, u32[]{:S(2)}) copy-start(f32[192,768]{1,0:T(8,128)} %param.28) | copy-start | bytes 1769476
  335.3 20.0 %copy-start.21 = (f32[768,192]{0,1:T(8,128)S(1)}, f32[768,192]{0,1:T(8,128)}, u32[]{:S(2)}) copy-start(f32[768,192]{0,1:T(8,128)} %copy-done.20) | copy-start | bytes 1769476
  335.3 16.1 %all-to-all-start.4 = ((f32[192,4,192]{2,0,1:T(8,128)}), f32[192,4,192]{2,0,1:T(8,128)}, u32[]{:S(2)}, u32[]{:S(2)}) async-start(f32[192,4,192]{2,0,1:T(8,128)} %copy.100), calls=%async_computation.4 | async-start | bytes 1572864 | tf_op jit(solution)/shard_map/all_to_all | solution.py:202
  339.7 177.2 %reduce-scatter.8.cloned.1.call-start = ((), (), s32[]{:S(2)}) async-start(), calls=%async_computation.22 | async-start | bytes 3538944 | tf_op jit(solution)/shard_map/reduce_scatter | solution.py:242
  482.0 108.9 %reduce-scatter.16.cloned.1.call-start = ((), (), s32[]{:S(2)}) async-start(), calls=%async_computation.26 | async-start | bytes 2654208 | tf_op jit(solution)/shard_map/reduce_scatter | solution.py:276
  486.8 127.8 %reduce-scatter.10.cloned.1.call-start = ((), (), s32[]{:S(2)}) async-start(), calls=%async_computation.23 | async-start | bytes 2654208 | tf_op jit(solution)/shard_map/reduce_scatter | solution.py:271
  487.1 16.0 %copy-start.34 = (f32[768]{0:T(1024)S(1)}, f32[768]{0:T(1024)}, u32[]{:S(2)}) copy-start(f32[768]{0:T(1024)} %copy-done.32) | copy-start | bytes 9220
  487.1 16.0 %copy-start.40 = (f32[768]{0:T(1024)S(1)}, f32[768]{0:T(1024)}, u32[]{:S(2)}) copy-start(f32[768]{0:T(1024)} %copy-done.38) | copy-start | bytes 9220
  487.1 16.0 %copy-start.45 = (f32[192]{0:T(256)S(1)}, f32[192]{0:T(256)}, u32[]{:S(2)}) copy-start(f32[192]{0:T(256)} %copy-done.43) | copy-start | bytes 2308
  487.1 16.0 %copy-start.50 = (f32[192]{0:T(256)S(1)}, f32[192]{0:T(256)}, u32[]{:S(2)}) copy-start(f32[192]{0:T(256)} %copy-done.48) | copy-start | bytes 2308
  506.8 154.0 %reduce-scatter.12.cloned.1.call-start = ((), (), s32[]{:S(2)}) async-start(), calls=%async_computation.24 | async-start | bytes 2654208 | tf_op jit(solution)/shard_map/reduce_scatter | solution.py:273
  538.9 167.7 %reduce-scatter.14.cloned.1.call-start = ((), (), s32[]{:S(2)}) async-start(), calls=%async_computation.25 | async-start | bytes 2654208 | tf_op jit(solution)/shard_map/reduce_scatter | solution.py:274
  566.3 220.7 %reduce-scatter.18.cloned.1.call-start = ((), (), s32[]{:S(2)}) async-start(), calls=%async_computation.27 | async-start | bytes 10616832 | tf_op jit(solution)/shard_map/reduce_scatter | solution.py:278
  577.4 289.8 %reduce-scatter.20.cloned.1.call-start = ((), (), s32[]{:S(2)}) async-start(), calls=%async_computation.28 | async-start | bytes 10616832 | tf_op jit(solution)/shard_map/reduce_scatter | solution.py:280
  590.8 278.4 %copy-start.61 = (f32[96]{0:T(128)S(1)}, f32[96]{0:T(128)}, u32[]{:S(2)}) copy-start(f32[96]{0:T(128)} %param.39) | copy-start | bytes 1156
  590.8 415.5 %all-reduce.23.cloned.1.call-start = ((), (), s32[]{:S(2)}) async-start(), calls=%async_computation.29 | async-start | bytes 7077888 | tf_op jit(solution)/shard_map/psum | solution.py:287
  (41 other events, 157.7 us)
Sparse Core Ops, SparseCore 0:
  9.9 32.0 all-gather.11
  43.9 30.6 all-gather.9
  76.5 31.5 all-gather.15
  110.1 36.0 all-gather.13
  147.9 29.0 all-gather.17
  178.8 66.0 all-gather.19
  246.8 57.9 all-gather.21
  482.1 34.7 reduce-scatter.7
  520.6 48.2 reduce-scatter.15
  572.1 42.4 reduce-scatter.9
  618.3 42.4 reduce-scatter.11
  664.0 42.4 reduce-scatter.13
  710.5 76.4 reduce-scatter.17
  790.7 76.4 reduce-scatter.19
  870.2 136.0 all-reduce.22
